TPU v7x, 256 devices: a whole 4x4x8 slice. The times are simulated.
256 devices in a mesh: dp: 4 (over x), ep: 64 (over y, z, core).
Axes of the slice: x: 4, y: 4, z: 8, core: 2. Of those that a mesh axis runs over, the one named last changes fastest.
Arguments:
- queries: bfloat16 [8192, 36864], P('ep', 'dp'), may hold values from -40 to 40
- suffix_latent: bfloat16 [8192, 576], P('ep'), may hold values from -10 to 10
- page_pool: bfloat16 [512, 36864], P('ep'), may hold values from -6 to 6
- page_owner: int32 [64, 32], P('ep'), may hold values from 0 to 63, as said below
- page_slot: int32 [64, 32], P('ep'), may hold values from 0 to 7
- prefix_len: int32 [64], P('ep'), may hold values from 1025 to 2048, as said below
- moe_input: bfloat16 [4096, 3584], P(('dp', 'ep')), may hold values from -6 to 6
- expert_ids: int32 [4096, 8], P(('dp', 'ep')), may hold values from 0 to 63, all different within a row; in each aligned block of 16 rows (0 to 15, 16 to 31, ...) at most 2 rows name the same one
- gate_weights: float32 [4096, 8], P(('dp', 'ep')), may hold values from 0.1 to 0.6
- w_gate: bfloat16 [64, 3584, 1024], P('ep', None, 'dp'), may hold values from -0.09375 to 0.09375
- w_up: bfloat16 [64, 3584, 1024], P('ep', None, 'dp'), may hold values from -0.09375 to 0.09375
- w_down: bfloat16 [64, 1024, 3584], P('ep', 'dp'), may hold values from -0.1875 to 0.1875
Outputs:
- attn_context: bfloat16 [8192, 32768], P('ep', 'dp')
- moe_output: bfloat16 [4096, 3584], P(('dp', 'ep'))
Inputs may be any that keep to these rules, and one draw needn't show every extreme that they name: `page_owner`: for a multiple m of the ep axis's size, the pages m, m + 1, ... of one request up to m + that size - 1 have distinct owners, so page k is the (k div that size)-th page of its request on its owner; entries past a request's prefix are valid page references too. `prefix_len`: some request has the longest prefix, 2048 tokens. `expert_ids`: in the 16 rows of one device no expert is named by more than 2 rows.
All inputs are finite; a program needn't handle non-finite values.
Results may differ from a plain program's by a relative error of at most 0.0057.
Values may be sent and summed in bfloat16 or wider, within the bound.
A program may use at most 128 MiB of HBM per device.

v0:
```python
import math

import jax
import jax.numpy as jnp
from jax import lax
from jax.experimental import pallas as pl
from jax.experimental.pallas import tpu as pltpu
from jax.sharding import PartitionSpec as P

LATENT = 512
KD = 576
PAGE = 64
SCALE = 0.07216878364870322
NEG = -1e30
LOG2E = 1.4426950408889634

NX = 4
NZ = 8
NG = 8
ROWS = 128
BLOCK = 16
REQ = 128
DISPATCH = (512, 512, 512, 1024, 1024)
PAGE_PARTS = 3
COMBINE = (1024, 1024, 512, 512, 512)
MESH = pl.DeviceIdType.MESH


def position():
    x = lax.axis_index("dp")
    ep = lax.axis_index("ep")
    core = lax.rem(ep, 2)
    z = lax.rem(lax.div(ep, 2), NZ)
    y = lax.div(ep, 2 * NZ)
    return x, y, z, core


def peers():
    x, y, z, core = position()
    g = y * 2 + core

    def along_z(d):
        other = lax.rem(z + d, NZ)
        return other, (x, (y * NZ + other) * 2 + core)

    def along_g(d):
        other = lax.rem(g + d, NG)
        return other, (x, (lax.div(other, 2) * NZ + z) * 2 + lax.rem(other, 2))

    def along_x(d):
        other = lax.rem(x + d, NX)
        return other, (other, (y * NZ + z) * 2 + core)

    return (x, z, g), (along_x, along_z, along_g)


def greet(along_x, along_z, along_g):
    barrier = pltpu.get_barrier_semaphore()

    def signal(dev):
        pl.semaphore_signal(barrier, inc=1, device_id=dev, device_id_type=MESH)

    def one(d, carry):
        signal(along_z(d)[1])
        signal(along_g(d)[1])
        return carry

    lax.fori_loop(1, 8, one, 0)
    signal(along_x(1)[1])
    signal(along_x(3)[1])
    return lambda: pl.semaphore_wait(barrier, 16)


def block_at(i):
    return pl.ds(pl.multiple_of(i * BLOCK, BLOCK), BLOCK)


def exchange(src, dst, cols, me, along, send_sem, recv_sem):
    def one(d, carry):
        other, dev = along(d)
        pltpu.make_async_remote_copy(
            src_ref=src.at[block_at(other), cols],
            dst_ref=dst.at[block_at(me), cols],
            send_sem=send_sem,
            recv_sem=recv_sem,
            device_id=dev,
            device_id_type=MESH,
        ).start()
        return carry

    lax.fori_loop(1, 8, one, 0)
    dst[block_at(me), cols] = src[block_at(me), cols]


def settle(ref, cols, sem):
    seven = ref.at[0 : 7 * BLOCK, cols]
    pltpu.make_async_copy(seven, seven, sem).wait()


def send(src, dst, send_sem, recv_sem, dev):
    copy = pltpu.make_async_remote_copy(
        src_ref=src, dst_ref=dst, send_sem=send_sem, recv_sem=recv_sem, device_id=dev, device_id_type=MESH
    )
    copy.start()
    return copy


def arrived(ref, sem):
    pltpu.make_async_copy(ref, ref, sem).wait()


def regroup():
    to = lax.broadcasted_iota(jnp.int32, (ROWS, ROWS), 0)
    of = lax.broadcasted_iota(jnp.int32, (ROWS, ROWS), 1)
    wanted = (lax.rem(to, 16) >> 1) * 16 + (to >> 4) * 2 + (to & 1)
    return jnp.where(of == wanted, 1.0, 0.0).astype(jnp.bfloat16)


def mm(a, b):
    return jnp.dot(a, b, preferred_element_type=jnp.float32)


def nt(a, b):
    return lax.dot_general(a, b, (((1,), (1,)), ((), ())), preferred_element_type=jnp.float32)


def iota(shape, dim):
    return lax.broadcasted_iota(jnp.int32, shape, dim)


def device_of(outer, inner, z_first):
    z, g = (outer, inner) if z_first else (inner, outer)
    return ((g >> 1) * NZ + z) * 2 + (g & 1)


def row_device(shape, dim, z_first):
    row = iota(shape, dim)
    return device_of(row >> 4, (row >> 1) & 7, z_first)


def identity(size):
    return jnp.where(iota((size, size), 0) == iota((size, size), 1), 1.0, 0.0).astype(jnp.bfloat16)


def spans(sizes, start=0):
    found = []
    for size in sizes:
        found.append(slice(start, start + size))
        start += size
    return found


def whole_kernel(
    length, ids, gates, owner, slot, tokens, pool_hbm, wg_hbm, wu_hbm, wd_hbm, q_hbm, suffix,
    context, out,
    rows, za, zb, xg, pool, ps, pza, pzb, pya, kg, wg, wu, wd, hidden,
    queries, qx, keys, causal,
    part_far, part_right, part_left, near_right, near_left, part_own, relay_left, relay_right, from_left, from_right,
    cy, cya, cz, cza,
    local, zs, zr, ys, yr, xs, xr, pzs, pzr, pys, pyr, pxs, pxr, rs, rr, cys, cyr, czs, czr,
):
    (x, z, g), (along_x, along_z, along_g) = peers()
    greeted = greet(along_x, along_z, along_g)
    bf, f32 = jnp.bfloat16, jnp.float32
    half_page = pool.shape[2]
    loads = [
        pltpu.make_async_copy(
            pool_hbm.at[:, pl.ds(pl.multiple_of(x * (2 * half_page) + i * half_page, 128), half_page)],
            pool.at[i],
            local.at[i],
        )
        for i in range(2)
    ]
    loads += [
        pltpu.make_async_copy(wg_hbm.at[0], wg, local.at[2]),
        pltpu.make_async_copy(wu_hbm.at[0], wu, local.at[3]),
        pltpu.make_async_copy(wd_hbm.at[0], wd, local.at[4]),
        pltpu.make_async_copy(q_hbm, queries, local.at[5]),
    ]
    for load in loads:
        load.start()
    tok_count, hid = tokens.shape
    out_chunks = spans([REQ + DISPATCH[0], *DISPATCH[1:]])
    own = spans(DISPATCH, REQ)
    page_chunks = spans([half_page // PAGE_PARTS] * PAGE_PARTS)
    cols = spans(COMBINE)
    right, to_right = along_x(1)
    left, to_left = along_x(3)
    far = lax.rem(x + 2, NX)
    mine = xg.at[x]
    perm = regroup()
    top, low = slice(0, 64), slice(64, 128)

    expert = row_device((ROWS, tok_count), 0, True)
    hits = [ids[k : k + 1, :] == expert for k in range(ids.shape[0])]
    named = hits[0]
    for hit in hits[1:]:
        named = named | hit
    below = (iota((tok_count, tok_count), 0) < iota((tok_count, tok_count), 1)).astype(f32).astype(bf)
    before = mm(named.astype(f32).astype(bf), below)
    placed = named & (before == (iota((ROWS, tok_count), 0) & 1).astype(f32))
    page_count = owner.shape[1]
    asks = owner[...] == row_device((ROWS, page_count), 0, True)
    asked = jnp.sum(jnp.where(asks, slot[...] + 1, 0), axis=1, keepdims=True)
    lane = iota((ROWS, REQ), 1)
    row = iota((ROWS, REQ), 0)
    req = (lane < 16) & ((lane & 7) + 1 == asked) & ((lane >> 3) == (row & 1))
    rows[:, 0:REQ] = req.astype(f32).astype(bf)
    rows[:, REQ:] = mm(placed.astype(f32).astype(bf), tokens[...]).astype(bf)
    greeted()
    for c in range(len(out_chunks)):
        exchange(rows, za, out_chunks[c], z, along_z, zs.at[c], zr.at[c])

    weight = jnp.zeros((ROWS, tok_count), f32)
    for k, hit in enumerate(hits):
        weight = weight + jnp.where(hit & placed, gates[k : k + 1, :], 0.0)
    gate_1 = weight.astype(bf)
    rest = weight - gate_1.astype(f32)
    gate_2 = rest.astype(bf)
    gate_3 = (rest - gate_2.astype(f32)).astype(bf)
    eye = identity(tok_count)
    gate_1, gate_2, gate_3 = (nt(eye, part).astype(bf) for part in (gate_1, gate_2, gate_3))
    holds = (owner[...] == row_device((ROWS, page_count), 0, False)).astype(f32).astype(bf)
    spread = ((iota((64, page_count), 0) >> 1) == iota((64, page_count), 1)).astype(f32).astype(bf)
    sel = jnp.where((iota((64, ROWS), 0) & 1) == (iota((64, ROWS), 1) & 1), nt(spread, holds), 0.0).astype(bf)

    def z_to_y(c):
        settle(za, out_chunks[c], zr.at[c])
        zb[:, out_chunks[c]] = mm(perm, za[:, out_chunks[c]]).astype(bf)
        exchange(zb, mine, out_chunks[c], g, along_g, ys.at[c], yr.at[c])

    def y_to_x(c):
        settle(mine, out_chunks[c], yr.at[c])
        part = xg.at[x, :, own[c]]
        send(part, part, xs.at[0, c], xr.at[0, c], to_right)
        send(part, part, xs.at[1, c], xr.at[1, c], to_left)

    def forward(c):
        arrived(xg.at[left, :, own[c]], xr.at[0, c])
        part = xg.at[left, top, own[c]]
        send(part, part, xs.at[2, c], xr.at[2, c], to_right)
        arrived(xg.at[right, :, own[c]], xr.at[1, c])
        part = xg.at[right, low, own[c]]
        send(part, part, xs.at[3, c], xr.at[3, c], to_left)

    def ask():
        wanted = mm(perm, xg[x, :, 0:REQ]).astype(bf)
        loads[0].wait()
        loads[1].wait()
        for c in range(PAGE_PARTS):
            ps[:, page_chunks[c]] = (
                mm(wanted[:, 0:8], pool[0, :, page_chunks[c]]) + mm(wanted[:, 8:16], pool[1, :, page_chunks[c]])
            ).astype(bf)
            exchange(ps, pza, page_chunks[c], z, along_z, pzs.at[c], pzr.at[c])

    def page_z_to_y(c):
        settle(pza, page_chunks[c], pzr.at[c])
        pzb[:, page_chunks[c]] = mm(perm, pza[:, page_chunks[c]]).astype(bf)
        exchange(pzb, pya, page_chunks[c], g, along_g, pys.at[c], pyr.at[c])

    def page_y_to_x(c):
        settle(pya, page_chunks[c], pyr.at[c])
        kg[x, :, page_chunks[c]] = mm(sel, pya[:, page_chunks[c]]).astype(bf)
        part = kg.at[x, :, page_chunks[c]]
        send(part, part, pxs.at[0, c], pxr.at[0, c], to_right)
        send(part, part, pxs.at[1, c], pxr.at[1, c], to_left)

    def page_forward(c):
        arrived(kg.at[left, :, page_chunks[c]], pxr.at[0, c])
        part = kg.at[left, 0:32, page_chunks[c]]
        send(part, part, pxs.at[2, c], pxr.at[2, c], to_right)
        arrived(kg.at[right, :, page_chunks[c]], pxr.at[1, c])
        part = kg.at[right, 32:64, page_chunks[c]]
        send(part, part, pxs.at[3, c], pxr.at[3, c], to_left)

    def ffn(group):
        taken = xg[group, :, REQ:]
        gate = mm(taken, wg[...])
        up = mm(taken, wu[...])
        hidden[group] = (gate / (1.0 + jnp.exp(-gate)) * up).astype(bf)

    def start_far(c):
        part_far[:, cols[c]] = mm(hidden[far], wd[:, cols[c]]).astype(bf)
        send(part_far.at[top, cols[c]], relay_left.at[:, cols[c]], rs.at[0, c], rr.at[0, c], to_right)
        send(part_far.at[low, cols[c]], relay_right.at[:, cols[c]], rs.at[1, c], rr.at[1, c], to_left)

    def start_near(c):
        part_right[:, cols[c]] = mm(hidden[right], wd[:, cols[c]])
        part_left[:, cols[c]] = mm(hidden[left], wd[:, cols[c]])
        near_right[low, cols[c]] = part_right[low, cols[c]].astype(bf)
        near_left[top, cols[c]] = part_left[top, cols[c]].astype(bf)
        send(near_right.at[low, cols[c]], from_left.at[low, cols[c]], rs.at[2, c], rr.at[2, c], to_right)
        send(near_left.at[top, cols[c]], from_right.at[top, cols[c]], rs.at[3, c], rr.at[3, c], to_left)
        part_own[:, cols[c]] = mm(hidden[x], wd[:, cols[c]])

    def relay(c):
        arrived(relay_left.at[:, cols[c]], rr.at[0, c])
        near_right[top, cols[c]] = (part_right[top, cols[c]] + relay_left[:, cols[c]].astype(f32)).astype(bf)
        send(near_right.at[top, cols[c]], from_left.at[top, cols[c]], rs.at[4, c], rr.at[4, c], to_right)
        arrived(relay_right.at[:, cols[c]], rr.at[1, c])
        near_left[low, cols[c]] = (part_left[low, cols[c]] + relay_right[:, cols[c]].astype(f32)).astype(bf)
        send(near_left.at[low, cols[c]], from_right.at[low, cols[c]], rs.at[5, c], rr.at[5, c], to_left)

    def to_y(c):
        arrived(from_left.at[low, cols[c]], rr.at[2, c])
        arrived(from_right.at[top, cols[c]], rr.at[3, c])
        arrived(from_left.at[top, cols[c]], rr.at[4, c])
        arrived(from_right.at[low, cols[c]], rr.at[5, c])
        cy[:, cols[c]] = (
            part_own[:, cols[c]] + from_left[:, cols[c]].astype(f32) + from_right[:, cols[c]].astype(f32)
        ).astype(bf)
        exchange(cy, cya, cols[c], g, along_g, cys.at[c], cyr.at[c])

    def to_z(c):
        settle(cya, cols[c], cyr.at[c])
        cz[:, cols[c]] = mm(perm, cya[:, cols[c]]).astype(bf)
        exchange(cz, cza, cols[c], z, along_z, czs.at[c], czr.at[c])

    def combine(c):
        settle(cza, cols[c], czr.at[c])
        back = cza[:, cols[c]]
        out[:, cols[c]] = (mm(gate_1, back) + mm(gate_2, back) + mm(gate_3, back)).astype(bf)

    def place_queries():
        loads[5].wait()
        one = jnp.where(iota((128, 64), 1) == 0, 1.0, 0.0).astype(bf)
        for h in range(16):
            qx[h * 128 : (h + 1) * 128, 0:KD] = queries[:, h * KD : (h + 1) * KD]
            qx[h * 128 : (h + 1) * 128, KD : KD + 64] = one
        causal[...] = jnp.where(iota((256, 128), 1) > (iota((256, 128), 0) & 127), NEG, 0.0)
        keys[2048:2176, 0:KD] = nt(identity(128), suffix[...]).astype(bf)
        keys[2048:2176, KD : KD + 64] = jnp.zeros((128, 64), bf)

    def gather_keys():
        lanes, line = iota((64, 64), 1), iota((64, 64), 0)
        for q in range(4):
            for j in range(8):
                at = slice((q * 8 + j) * 64, (q * 8 + j + 1) * 64)
                keys[at, 0:KD] = kg[q, :, j * KD : (j + 1) * KD]
                place = (line >> 1) * PAGE + q * 16 + (line & 1) * 8 + j
                keys[at, KD : KD + 64] = jnp.where((lanes == 0) & (place >= length[0]), NEG, 0.0).astype(bf)

    def attend(i):
        q = qx[pl.ds(pl.multiple_of(i * 256, 256), 256), :]
        near = nt(q, keys[2048:2176, :]) + causal[...]
        past = nt(q, keys[0:2048, :])
        peak = jnp.maximum(jnp.max(past, axis=1, keepdims=True), jnp.max(near, axis=1, keepdims=True))
        shift = peak * (SCALE * LOG2E)
        past = jnp.exp2(past * (SCALE * LOG2E) - shift)
        near = jnp.exp2(near * (SCALE * LOG2E) - shift)
        total = jnp.sum(past, axis=1, keepdims=True) + jnp.sum(near, axis=1, keepdims=True)
        got = mm(past.astype(bf), keys[0:2048, 0:LATENT]) + mm(near.astype(bf), keys[2048:2176, 0:LATENT])
        got = (got / total).astype(bf)
        at = pl.multiple_of(i * 1024, 1024)
        context[:, pl.ds(at, 512)] = got[0:128]
        context[:, pl.ds(at + 512, 512)] = got[128:256]

    def wait_far():
        for c in range(len(own)):
            arrived(xg.at[far, top, own[c]], xr.at[2, c])
            arrived(xg.at[far, low, own[c]], xr.at[3, c])

    def wait_keys():
        for c in range(PAGE_PARTS):
            arrived(kg.at[far, 0:32, page_chunks[c]], pxr.at[2, c])
            arrived(kg.at[far, 32:64, page_chunks[c]], pxr.at[3, c])

    def wait_weights():
        for i in (2, 3, 4):
            loads[i].wait()

    z_to_y(0)
    y_to_x(0)
    z_to_y(1)
    y_to_x(1)
    z_to_y(2)
    place_queries()
    forward(0)
    y_to_x(2)
    z_to_y(3)
    forward(1)
    ask()
    y_to_x(3)
    z_to_y(4)
    y_to_x(4)
    forward(2)
    page_z_to_y(0)
    forward(3)
    page_y_to_x(0)
    page_z_to_y(1)
    forward(4)
    page_forward(0)
    wait_weights()
    ffn(right)
    wait_far()
    page_y_to_x(1)
    page_z_to_y(2)
    ffn(left)
    ffn(x)
    ffn(far)
    start_far(0)
    page_y_to_x(2)
    page_forward(1)
    page_forward(2)
    start_near(0)
    relay(0)
    start_far(1)
    start_near(1)
    wait_keys()
    gather_keys()

    def beside_2():
        to_y(0)
        relay(1)
        start_far(2)

    def beside_3():
        start_far(3)
        start_near(2)
        to_z(0)
        start_far(4)
        to_y(1)

    def beside_4():
        relay(2)
        start_near(3)
        relay(3)
        to_z(1)
        start_near(4)
        relay(4)
        to_y(2)

    def beside_5():
        combine(0)
        to_z(2)
        to_y(3)
        to_y(4)
        to_z(3)
        combine(1)
        to_z(4)

    def beside_6():
        combine(2)
        combine(3)

    @pl.loop(0, 8)
    def _(i):
        attend(i)
        pl.when(i == 2)(beside_2)
        pl.when(i == 3)(beside_3)
        pl.when(i == 4)(beside_4)
        pl.when(i == 5)(beside_5)
        pl.when(i == 6)(beside_6)

    combine(4)
    for c in range(len(own)):
        settle(rows, out_chunks[c], zs.at[c])
        settle(zb, out_chunks[c], ys.at[c])
        arrived(xg.at[x, :, own[c]], xs.at[0, c])
        arrived(xg.at[x, :, own[c]], xs.at[1, c])
        arrived(xg.at[left, top, own[c]], xs.at[2, c])
        arrived(xg.at[right, low, own[c]], xs.at[3, c])
    for c in range(len(cols)):
        settle(cy, cols[c], cys.at[c])
        settle(cz, cols[c], czs.at[c])
        arrived(part_far.at[top, cols[c]], rs.at[0, c])
        arrived(part_far.at[low, cols[c]], rs.at[1, c])
        arrived(near_right.at[low, cols[c]], rs.at[2, c])
        arrived(near_left.at[top, cols[c]], rs.at[3, c])
        arrived(near_right.at[top, cols[c]], rs.at[4, c])
        arrived(near_left.at[low, cols[c]], rs.at[5, c])
    for c in range(PAGE_PARTS):
        settle(ps, page_chunks[c], pzs.at[c])
        settle(pzb, page_chunks[c], pys.at[c])
        arrived(kg.at[x, :, page_chunks[c]], pxs.at[0, c])
        arrived(kg.at[x, :, page_chunks[c]], pxs.at[1, c])
        arrived(kg.at[left, 0:32, page_chunks[c]], pxs.at[2, c])
        arrived(kg.at[right, 32:64, page_chunks[c]], pxs.at[3, c])


def on_device(
    queries,
    suffix_latent,
    page_pool,
    page_owner,
    page_slot,
    prefix_len,
    moe_input,
    expert_ids,
    gate_weights,
    w_gate,
    w_up,
    w_down,
):
    bf, f32 = jnp.bfloat16, jnp.float32
    hid, unit = w_gate.shape[1:]
    wide = page_pool.shape[1] // (2 * NX)
    vmem = pl.BlockSpec(memory_space=pltpu.VMEM)
    hbm = pl.BlockSpec(memory_space=pltpu.HBM)
    dma = pltpu.SemaphoreType.DMA
    d, p, n = len(DISPATCH), PAGE_PARTS, len(COMBINE)
    new, heads = queries.shape[0], queries.shape[1] // KD
    full, paged = pltpu.VMEM((ROWS, hid), bf), pltpu.VMEM((ROWS, wide), bf)
    asking = pltpu.VMEM((ROWS, REQ + hid), bf)
    return pl.pallas_call(
        whole_kernel,
        out_shape=(
            pltpu.VMEM((new, heads * LATENT), bf),
            pltpu.VMEM(moe_input.shape, bf),
        ),
        in_specs=[pl.BlockSpec(memory_space=pltpu.SMEM)] + [vmem] * 5 + [hbm] * 5 + [vmem],
        out_specs=(vmem, vmem),
        scratch_shapes=[
            asking, asking, asking,
            pltpu.VMEM((NX, ROWS, REQ + hid), bf),
            pltpu.VMEM((2, page_pool.shape[0], wide), bf),
            paged, paged, paged, paged,
            pltpu.VMEM((NX, 64, wide), bf),
            pltpu.VMEM((hid, unit), bf), pltpu.VMEM((hid, unit), bf), pltpu.VMEM((unit, hid), bf),
            pltpu.VMEM((NX, ROWS, unit), bf),
            pltpu.VMEM(queries.shape, bf),
            pltpu.VMEM((2048, 640), bf),
            pltpu.VMEM((2176, 640), bf),
            pltpu.VMEM((256, 128), f32),
            full, pltpu.VMEM((ROWS, hid), f32), pltpu.VMEM((ROWS, hid), f32), full, full, pltpu.VMEM((ROWS, hid), f32),
            pltpu.VMEM((64, hid), bf), pltpu.VMEM((64, hid), bf), full, full,
            full, full, full, full,
            dma((6,)),
            dma((d,)), dma((d,)), dma((d,)), dma((d,)), dma((4, d)), dma((4, d)),
            dma((p,)), dma((p,)), dma((p,)), dma((p,)), dma((4, p)), dma((4, p)),
            dma((6, n)), dma((6, n)), dma((n,)), dma((n,)), dma((n,)), dma((n,)),
        ],
        compiler_params=pltpu.CompilerParams(
            collective_id=0, has_side_effects=True, vmem_limit_bytes=52 * 2**20
        ),
        name="whole",
    )(
        prefix_len, expert_ids.T, gate_weights.T, page_owner, page_slot, moe_input,
        page_pool, w_gate, w_up, w_down, queries, suffix_latent.T,
    )


def solution(mesh):
    return jax.shard_map(
        on_device,
        mesh=mesh,
        in_specs=(
            P("ep", "dp"),
            P("ep", None),
            P("ep", None),
            P("ep", None),
            P("ep", None),
            P("ep"),
            P(("dp", "ep"), None),
            P(("dp", "ep"), None),
            P(("dp", "ep"), None),
            P("ep", None, "dp"),
            P("ep", None, "dp"),
            P("ep", "dp", None),
        ),
        out_specs=(P("ep", "dp"), P(("dp", "ep"), None)),
        check_vma=False,
    )
```

profile of v0, /device:TPU:1, one launch (start us, length us, event | category | flops | bytes accessed | tf_op | source)
XLA Modules:
  0.0 126.4 jit_solution(13331601066707881498)
XLA Ops:
  1.3 123.1 %whole.1 = (bf16[128,8192]{1,0:T(8,128)(2,1)S(1)}, bf16[16,3584]{1,0:T(8,128)(2,1)S(1)}) custom-call(s32[1]{0:T(128)S(6)} %copy.18.length, s32[8,16]{1,0:T(8,128)} %bitcast.4, f32[8,16]{1,0:T(8,128)} %bitcast.5, s32[1,32]{1,0:T(1,128)} %owner.1, s32[1,32]{1,0:T(1,128)} %slot.1, bf16[16,3584]{1,0:T(8,128)(2,1)} %tokens.1, bf16[8,36864]{1,0:T(8,128)(2,1)} %pool_hbm.1, ...), custom_call_target="tpu_custom_call" | custom-call | tf_op jit(solution)/shard_map/whole/pallas_call | solution.py:505
  124.4 1.3 %copy.16 = bf16[128,8192]{1,0:T(8,128)(2,1)} copy(bf16[128,8192]{1,0:T(8,128)(2,1)S(1)} %get-tuple-element.2) | data formatting | bytes 4194304
  125.7 0.6 copy.17
where the time goes:
time: 126 us
  Pallas kernels  123 us (98%)
  local copies, waits for them, and re-layouts  1.97 us (2%)
  between operations  1.29 us (1%)
    pallas_call x1, Pallas kernels, on_device(): pl.pallas_call(whole_kernel, out_shape=(pltpu.VMEM((new, heads * LATENT),...  123 us

commit v1 on v0

--- a/solution.py
+++ b/solution.py
@@ -21,8 +21,9 @@
 BLOCK = 16
 REQ = 128
 DISPATCH = (512, 512, 512, 1024, 1024)
-PAGE_PARTS = 3
-COMBINE = (1024, 1024, 512, 512, 512)
+PAGES = (1152, 1152, 1152, 1152)
+FIRST = 6
+COMBINE = (1024, 1024, 768, 512, 256)
 MESH = pl.DeviceIdType.MESH
 
 
@@ -154,7 +155,7 @@
     length, ids, gates, owner, slot, tokens, pool_hbm, wg_hbm, wu_hbm, wd_hbm, q_hbm, suffix,
     context, out,
     rows, za, zb, xg, pool, ps, pza, pzb, pya, kg, wg, wu, wd, hidden,
-    queries, qx, keys, causal,
+    queries, qx, keys, causal, partial, stats,
     part_far, part_right, part_left, near_right, near_left, part_own, relay_left, relay_right, from_left, from_right,
     cy, cya, cz, cza,
     local, zs, zr, ys, yr, xs, xr, pzs, pzr, pys, pyr, pxs, pxr, rs, rr, cys, cyr, czs, czr,
@@ -180,9 +181,11 @@
     for load in loads:
         load.start()
     tok_count, hid = tokens.shape
-    out_chunks = spans([REQ + DISPATCH[0], *DISPATCH[1:]])
-    own = spans(DISPATCH, REQ)
-    page_chunks = spans([half_page // PAGE_PARTS] * PAGE_PARTS)
+    own = spans((DISPATCH[0], *DISPATCH[2:], DISPATCH[1]))
+    own = [own[0], own[-1], *own[1:-1]]
+    out_chunks = [own[0], slice(own[1].start, hid + REQ), *own[2:]]
+    page_chunks = spans(PAGES)
+    firsts = next(i for i in range(len(PAGES) + 1) if sum(PAGES[:i]) >= FIRST * KD)
     cols = spans(COMBINE)
     right, to_right = along_x(1)
     left, to_left = along_x(3)
@@ -205,11 +208,11 @@
     lane = iota((ROWS, REQ), 1)
     row = iota((ROWS, REQ), 0)
     req = (lane < 16) & ((lane & 7) + 1 == asked) & ((lane >> 3) == (row & 1))
-    rows[:, 0:REQ] = req.astype(f32).astype(bf)
-    rows[:, REQ:] = mm(placed.astype(f32).astype(bf), tokens[...]).astype(bf)
+    rows[:, hid:] = req.astype(f32).astype(bf)
+    rows[:, 0:hid] = mm(placed.astype(f32).astype(bf), tokens[...]).astype(bf)
     greeted()
     for c in range(len(out_chunks)):
-        exchange(rows, za, out_chunks[c], z, along_z, zs.at[c], zr.at[c])
+        exchange(rows, za, out_chunks[c], z, along_z, zs.at[0], zr.at[c])
 
     weight = jnp.zeros((ROWS, tok_count), f32)
     for k, hit in enumerate(hits):
@@ -227,94 +230,96 @@
     def z_to_y(c):
         settle(za, out_chunks[c], zr.at[c])
         zb[:, out_chunks[c]] = mm(perm, za[:, out_chunks[c]]).astype(bf)
-        exchange(zb, mine, out_chunks[c], g, along_g, ys.at[c], yr.at[c])
+        exchange(zb, mine, out_chunks[c], g, along_g, ys.at[0], yr.at[c])
 
     def y_to_x(c):
         settle(mine, out_chunks[c], yr.at[c])
         part = xg.at[x, :, own[c]]
-        send(part, part, xs.at[0, c], xr.at[0, c], to_right)
-        send(part, part, xs.at[1, c], xr.at[1, c], to_left)
+        send(part, part, xs.at[0], xr.at[0, c], to_right)
+        send(part, part, xs.at[1], xr.at[1, c], to_left)
 
     def forward(c):
         arrived(xg.at[left, :, own[c]], xr.at[0, c])
         part = xg.at[left, top, own[c]]
-        send(part, part, xs.at[2, c], xr.at[2, c], to_right)
+        send(part, part, xs.at[2], xr.at[2, 0], to_right)
         arrived(xg.at[right, :, own[c]], xr.at[1, c])
         part = xg.at[right, low, own[c]]
-        send(part, part, xs.at[3, c], xr.at[3, c], to_left)
+        send(part, part, xs.at[3], xr.at[2, 0], to_left)
 
     def ask():
-        wanted = mm(perm, xg[x, :, 0:REQ]).astype(bf)
+        wanted = mm(perm, xg[x, :, hid:]).astype(bf)
         loads[0].wait()
         loads[1].wait()
-        for c in range(PAGE_PARTS):
+        for c in range(len(PAGES)):
             ps[:, page_chunks[c]] = (
                 mm(wanted[:, 0:8], pool[0, :, page_chunks[c]]) + mm(wanted[:, 8:16], pool[1, :, page_chunks[c]])
             ).astype(bf)
-            exchange(ps, pza, page_chunks[c], z, along_z, pzs.at[c], pzr.at[c])
+            exchange(ps, pza, page_chunks[c], z, along_z, pzs.at[0], pzr.at[c])
 
     def page_z_to_y(c):
         settle(pza, page_chunks[c], pzr.at[c])
         pzb[:, page_chunks[c]] = mm(perm, pza[:, page_chunks[c]]).astype(bf)
-        exchange(pzb, pya, page_chunks[c], g, along_g, pys.at[c], pyr.at[c])
+        exchange(pzb, pya, page_chunks[c], g, along_g, pys.at[0], pyr.at[c])
 
     def page_y_to_x(c):
         settle(pya, page_chunks[c], pyr.at[c])
         kg[x, :, page_chunks[c]] = mm(sel, pya[:, page_chunks[c]]).astype(bf)
         part = kg.at[x, :, page_chunks[c]]
-        send(part, part, pxs.at[0, c], pxr.at[0, c], to_right)
-        send(part, part, pxs.at[1, c], pxr.at[1, c], to_left)
+        send(part, part, pxs.at[0], pxr.at[0, c], to_right)
+        send(part, part, pxs.at[1], pxr.at[1, c], to_left)
 
     def page_forward(c):
         arrived(kg.at[left, :, page_chunks[c]], pxr.at[0, c])
         part = kg.at[left, 0:32, page_chunks[c]]
-        send(part, part, pxs.at[2, c], pxr.at[2, c], to_right)
+        send(part, part, pxs.at[2], pxr.at[2, c], to_right)
         arrived(kg.at[right, :, page_chunks[c]], pxr.at[1, c])
         part = kg.at[right, 32:64, page_chunks[c]]
-        send(part, part, pxs.at[3, c], pxr.at[3, c], to_left)
+        send(part, part, pxs.at[3], pxr.at[2, c], to_left)
 
     def ffn(group):
-        taken = xg[group, :, REQ:]
+        taken = xg[group, :, 0:hid]
         gate = mm(taken, wg[...])
         up = mm(taken, wu[...])
         hidden[group] = (gate / (1.0 + jnp.exp(-gate)) * up).astype(bf)
 
-    def start_far(c):
+    def calc_far(c):
         part_far[:, cols[c]] = mm(hidden[far], wd[:, cols[c]]).astype(bf)
-        send(part_far.at[top, cols[c]], relay_left.at[:, cols[c]], rs.at[0, c], rr.at[0, c], to_right)
-        send(part_far.at[low, cols[c]], relay_right.at[:, cols[c]], rs.at[1, c], rr.at[1, c], to_left)
-
-    def start_near(c):
+
+    def calc_near(c):
         part_right[:, cols[c]] = mm(hidden[right], wd[:, cols[c]])
         part_left[:, cols[c]] = mm(hidden[left], wd[:, cols[c]])
         near_right[low, cols[c]] = part_right[low, cols[c]].astype(bf)
         near_left[top, cols[c]] = part_left[top, cols[c]].astype(bf)
-        send(near_right.at[low, cols[c]], from_left.at[low, cols[c]], rs.at[2, c], rr.at[2, c], to_right)
-        send(near_left.at[top, cols[c]], from_right.at[top, cols[c]], rs.at[3, c], rr.at[3, c], to_left)
         part_own[:, cols[c]] = mm(hidden[x], wd[:, cols[c]])
+
+    def start_far(c):
+        send(part_far.at[top, cols[c]], relay_left.at[:, cols[c]], rs.at[0], rr.at[0, c], to_right)
+        send(part_far.at[low, cols[c]], relay_right.at[:, cols[c]], rs.at[1], rr.at[1, c], to_left)
+
+    def start_near(c):
+        send(near_right.at[low, cols[c]], from_left.at[low, cols[c]], rs.at[2], rr.at[2, c], to_right)
+        send(near_left.at[top, cols[c]], from_right.at[top, cols[c]], rs.at[3], rr.at[3, c], to_left)
 
     def relay(c):
         arrived(relay_left.at[:, cols[c]], rr.at[0, c])
         near_right[top, cols[c]] = (part_right[top, cols[c]] + relay_left[:, cols[c]].astype(f32)).astype(bf)
-        send(near_right.at[top, cols[c]], from_left.at[top, cols[c]], rs.at[4, c], rr.at[4, c], to_right)
+        send(near_right.at[top, cols[c]], from_left.at[top, cols[c]], rs.at[4], rr.at[2, c], to_right)
         arrived(relay_right.at[:, cols[c]], rr.at[1, c])
         near_left[low, cols[c]] = (part_left[low, cols[c]] + relay_right[:, cols[c]].astype(f32)).astype(bf)
-        send(near_left.at[low, cols[c]], from_right.at[low, cols[c]], rs.at[5, c], rr.at[5, c], to_left)
+        send(near_left.at[low, cols[c]], from_right.at[low, cols[c]], rs.at[5], rr.at[3, c], to_left)
 
     def to_y(c):
-        arrived(from_left.at[low, cols[c]], rr.at[2, c])
-        arrived(from_right.at[top, cols[c]], rr.at[3, c])
-        arrived(from_left.at[top, cols[c]], rr.at[4, c])
-        arrived(from_right.at[low, cols[c]], rr.at[5, c])
+        arrived(from_left.at[:, cols[c]], rr.at[2, c])
+        arrived(from_right.at[:, cols[c]], rr.at[3, c])
         cy[:, cols[c]] = (
             part_own[:, cols[c]] + from_left[:, cols[c]].astype(f32) + from_right[:, cols[c]].astype(f32)
         ).astype(bf)
-        exchange(cy, cya, cols[c], g, along_g, cys.at[c], cyr.at[c])
+        exchange(cy, cya, cols[c], g, along_g, cys.at[0], cyr.at[c])
 
     def to_z(c):
         settle(cya, cols[c], cyr.at[c])
         cz[:, cols[c]] = mm(perm, cya[:, cols[c]]).astype(bf)
-        exchange(cz, cza, cols[c], z, along_z, czs.at[c], czr.at[c])
+        exchange(cz, cza, cols[c], z, along_z, czs.at[0], czr.at[c])
 
     def combine(c):
         settle(cza, cols[c], czr.at[c])
@@ -331,151 +336,192 @@
         keys[2048:2176, 0:KD] = nt(identity(128), suffix[...]).astype(bf)
         keys[2048:2176, KD : KD + 64] = jnp.zeros((128, 64), bf)
 
-    def gather_keys():
+    def gather_keys(begin, end):
         lanes, line = iota((64, 64), 1), iota((64, 64), 0)
-        for q in range(4):
-            for j in range(8):
-                at = slice((q * 8 + j) * 64, (q * 8 + j + 1) * 64)
+        for j in range(begin, end):
+            for q in range(4):
+                at = slice((j * 4 + q) * 64, (j * 4 + q + 1) * 64)
                 keys[at, 0:KD] = kg[q, :, j * KD : (j + 1) * KD]
                 place = (line >> 1) * PAGE + q * 16 + (line & 1) * 8 + j
                 keys[at, KD : KD + 64] = jnp.where((lanes == 0) & (place >= length[0]), NEG, 0.0).astype(bf)
 
-    def attend(i):
-        q = qx[pl.ds(pl.multiple_of(i * 256, 256), 256), :]
+    split = FIRST * 256
+    tempo = SCALE * LOG2E
+
+    def attend_first(i):
+        at = pl.ds(pl.multiple_of(i * 256, 256), 256)
+        q = qx[at, :]
         near = nt(q, keys[2048:2176, :]) + causal[...]
-        past = nt(q, keys[0:2048, :])
-        peak = jnp.maximum(jnp.max(past, axis=1, keepdims=True), jnp.max(near, axis=1, keepdims=True))
-        shift = peak * (SCALE * LOG2E)
-        past = jnp.exp2(past * (SCALE * LOG2E) - shift)
-        near = jnp.exp2(near * (SCALE * LOG2E) - shift)
-        total = jnp.sum(past, axis=1, keepdims=True) + jnp.sum(near, axis=1, keepdims=True)
-        got = mm(past.astype(bf), keys[0:2048, 0:LATENT]) + mm(near.astype(bf), keys[2048:2176, 0:LATENT])
+        past = nt(q, keys[0:split, :])
+        peak = jnp.maximum(jnp.max(past, axis=1, keepdims=True), jnp.max(near, axis=1, keepdims=True)) * tempo
+        past = jnp.exp2(past * tempo - peak)
+        near = jnp.exp2(near * tempo - peak)
+        stats[at, 0:1] = peak
+        stats[at, 1:2] = jnp.sum(past, axis=1, keepdims=True) + jnp.sum(near, axis=1, keepdims=True)
+        partial[at, :] = mm(past.astype(bf), keys[0:split, 0:LATENT]) + mm(
+            near.astype(bf), keys[2048:2176, 0:LATENT]
+        )
+
+    def attend_second(i):
+        at = pl.ds(pl.multiple_of(i * 256, 256), 256)
+        q = qx[at, :]
+        past = nt(q, keys[split:2048, :])
+        was = stats[at, 0:1]
+        peak = jnp.maximum(jnp.max(past, axis=1, keepdims=True) * tempo, was)
+        past = jnp.exp2(past * tempo - peak)
+        fade = jnp.exp2(was - peak)
+        total = stats[at, 1:2] * fade + jnp.sum(past, axis=1, keepdims=True)
+        got = mm(past.astype(bf), keys[split:2048, 0:LATENT]) + partial[at, :] * fade
         got = (got / total).astype(bf)
-        at = pl.multiple_of(i * 1024, 1024)
-        context[:, pl.ds(at, 512)] = got[0:128]
-        context[:, pl.ds(at + 512, 512)] = got[128:256]
+        to = pl.multiple_of(i * 1024, 1024)
+        context[:, pl.ds(to, 512)] = got[0:128]
+        context[:, pl.ds(to + 512, 512)] = got[128:256]
 
     def wait_far():
-        for c in range(len(own)):
-            arrived(xg.at[far, top, own[c]], xr.at[2, c])
-            arrived(xg.at[far, low, own[c]], xr.at[3, c])
-
-    def wait_keys():
-        for c in range(PAGE_PARTS):
-            arrived(kg.at[far, 0:32, page_chunks[c]], pxr.at[2, c])
-            arrived(kg.at[far, 32:64, page_chunks[c]], pxr.at[3, c])
+        arrived(xg.at[far, :, 0:hid], xr.at[2, 0])
+
+    def wait_keys(begin, end):
+        for c in range(begin, end):
+            arrived(kg.at[far, :, page_chunks[c]], pxr.at[2, c])
 
     def wait_weights():
         for i in (2, 3, 4):
             loads[i].wait()
 
+    def drain_dispatch():
+        settle(rows, slice(0, hid + REQ), zs.at[0])
+        settle(zb, slice(0, hid + REQ), ys.at[0])
+        arrived(xg.at[x, :, 0:hid], xs.at[0])
+        arrived(xg.at[x, :, 0:hid], xs.at[1])
+        arrived(xg.at[left, top, 0:hid], xs.at[2])
+        arrived(xg.at[right, low, 0:hid], xs.at[3])
+        settle(ps, slice(0, half_page), pzs.at[0])
+
+    def drain():
+        settle(pzb, slice(0, half_page), pys.at[0])
+        arrived(kg.at[x], pxs.at[0])
+        arrived(kg.at[x], pxs.at[1])
+        arrived(kg.at[left, 0:32], pxs.at[2])
+        arrived(kg.at[right, 32:64], pxs.at[3])
+        arrived(part_far.at[top], rs.at[0])
+        arrived(part_far.at[low], rs.at[1])
+        arrived(near_right.at[low], rs.at[2])
+        arrived(near_left.at[top], rs.at[3])
+        arrived(near_right.at[top], rs.at[4])
+        arrived(near_left.at[low], rs.at[5])
+        settle(cy, slice(0, hid), cys.at[0])
+        settle(cz, slice(0, hid), czs.at[0])
+
     z_to_y(0)
+    z_to_y(1)
     y_to_x(0)
-    z_to_y(1)
+    z_to_y(2)
     y_to_x(1)
-    z_to_y(2)
-    place_queries()
+    y_to_x(2)
     forward(0)
-    y_to_x(2)
     z_to_y(3)
     forward(1)
     ask()
+    forward(2)
     y_to_x(3)
     z_to_y(4)
+    place_queries()
     y_to_x(4)
-    forward(2)
+    forward(3)
+    wait_weights()
+    ffn(x)
     page_z_to_y(0)
-    forward(3)
-    page_y_to_x(0)
     page_z_to_y(1)
     forward(4)
+    ffn(right)
+    page_y_to_x(0)
+    ffn(left)
+    page_z_to_y(2)
+    page_y_to_x(1)
+    wait_far()
     page_forward(0)
-    wait_weights()
-    ffn(right)
-    wait_far()
-    page_y_to_x(1)
-    page_z_to_y(2)
-    ffn(left)
-    ffn(x)
     ffn(far)
+    calc_far(0)
+    page_y_to_x(2)
     start_far(0)
-    page_y_to_x(2)
+    calc_near(0)
+    calc_far(1)
     page_forward(1)
+    calc_near(1)
+    page_z_to_y(3)
+    calc_far(2)
     page_forward(2)
+    calc_near(2)
+    calc_near(3)
+    start_far(1)
     start_near(0)
+    calc_far(3)
     relay(0)
-    start_far(1)
+    drain_dispatch()
+    wait_keys(0, firsts)
     start_near(1)
-    wait_keys()
-    gather_keys()
-
-    def beside_2():
-        to_y(0)
+    gather_keys(0, FIRST)
+    def first_0():
+        calc_near(4)
         relay(1)
         start_far(2)
 
-    def beside_3():
+    def first_1():
+        start_near(2)
+
+    def first_3():
+        to_y(0)
         start_far(3)
-        start_near(2)
+
+    def first_5():
+        to_y(1)
+        start_near(3)
         to_z(0)
+        calc_far(4)
+        relay(2)
+
+    def first_6():
         start_far(4)
-        to_y(1)
-
-    def beside_4():
-        relay(2)
-        start_near(3)
         relay(3)
+        page_y_to_x(3)
+        start_near(4)
         to_z(1)
-        start_near(4)
+        to_y(2)
         relay(4)
-        to_y(2)
-
-    def beside_5():
-        combine(0)
-        to_z(2)
         to_y(3)
-        to_y(4)
-        to_z(3)
-        combine(1)
-        to_z(4)
-
-    def beside_6():
-        combine(2)
-        combine(3)
 
     @pl.loop(0, 8)
     def _(i):
-        attend(i)
-        pl.when(i == 2)(beside_2)
-        pl.when(i == 3)(beside_3)
-        pl.when(i == 4)(beside_4)
-        pl.when(i == 5)(beside_5)
-        pl.when(i == 6)(beside_6)
-
+        attend_first(i)
+        pl.when(i == 0)(first_0)
+        pl.when(i == 1)(first_1)
+        pl.when(i == 3)(first_3)
+        pl.when(i == 5)(first_5)
+        pl.when(i == 6)(first_6)
+
+    page_forward(3)
+    to_z(2)
+    combine(0)
+    to_y(4)
+    to_z(3)
+    combine(1)
+    wait_keys(firsts, len(PAGES))
+    gather_keys(FIRST, 8)
+    def second_1():
+        to_z(4)
+
+    def second_4():
+        combine(2)
+
+    @pl.loop(0, 8)
+    def _(i):
+        attend_second(i)
+        pl.when(i == 1)(second_1)
+        pl.when(i == 4)(second_4)
+
+    combine(3)
     combine(4)
-    for c in range(len(own)):
-        settle(rows, out_chunks[c], zs.at[c])
-        settle(zb, out_chunks[c], ys.at[c])
-        arrived(xg.at[x, :, own[c]], xs.at[0, c])
-        arrived(xg.at[x, :, own[c]], xs.at[1, c])
-        arrived(xg.at[left, top, own[c]], xs.at[2, c])
-        arrived(xg.at[right, low, own[c]], xs.at[3, c])
-    for c in range(len(cols)):
-        settle(cy, cols[c], cys.at[c])
-        settle(cz, cols[c], czs.at[c])
-        arrived(part_far.at[top, cols[c]], rs.at[0, c])
-        arrived(part_far.at[low, cols[c]], rs.at[1, c])
-        arrived(near_right.at[low, cols[c]], rs.at[2, c])
-        arrived(near_left.at[top, cols[c]], rs.at[3, c])
-        arrived(near_right.at[top, cols[c]], rs.at[4, c])
-        arrived(near_left.at[low, cols[c]], rs.at[5, c])
-    for c in range(PAGE_PARTS):
-        settle(ps, page_chunks[c], pzs.at[c])
-        settle(pzb, page_chunks[c], pys.at[c])
-        arrived(kg.at[x, :, page_chunks[c]], pxs.at[0, c])
-        arrived(kg.at[x, :, page_chunks[c]], pxs.at[1, c])
-        arrived(kg.at[left, 0:32, page_chunks[c]], pxs.at[2, c])
-        arrived(kg.at[right, 32:64, page_chunks[c]], pxs.at[3, c])
+    drain()
 
 
 def on_device(
@@ -498,7 +544,7 @@
     vmem = pl.BlockSpec(memory_space=pltpu.VMEM)
     hbm = pl.BlockSpec(memory_space=pltpu.HBM)
     dma = pltpu.SemaphoreType.DMA
-    d, p, n = len(DISPATCH), PAGE_PARTS, len(COMBINE)
+    d, p, n = len(DISPATCH), len(PAGES), len(COMBINE)
     new, heads = queries.shape[0], queries.shape[1] // KD
     full, paged = pltpu.VMEM((ROWS, hid), bf), pltpu.VMEM((ROWS, wide), bf)
     asking = pltpu.VMEM((ROWS, REQ + hid), bf)
@@ -522,16 +568,18 @@
             pltpu.VMEM((2048, 640), bf),
             pltpu.VMEM((2176, 640), bf),
             pltpu.VMEM((256, 128), f32),
+            pltpu.VMEM((2048, LATENT), f32),
+            pltpu.VMEM((2048, 128), f32),
             full, pltpu.VMEM((ROWS, hid), f32), pltpu.VMEM((ROWS, hid), f32), full, full, pltpu.VMEM((ROWS, hid), f32),
             pltpu.VMEM((64, hid), bf), pltpu.VMEM((64, hid), bf), full, full,
             full, full, full, full,
             dma((6,)),
-            dma((d,)), dma((d,)), dma((d,)), dma((d,)), dma((4, d)), dma((4, d)),
-            dma((p,)), dma((p,)), dma((p,)), dma((p,)), dma((4, p)), dma((4, p)),
-            dma((6, n)), dma((6, n)), dma((n,)), dma((n,)), dma((n,)), dma((n,)),
+            dma((1,)), dma((d,)), dma((1,)), dma((d,)), dma((4,)), dma((3, d)),
+            dma((1,)), dma((p,)), dma((1,)), dma((p,)), dma((4,)), dma((3, p)),
+            dma((6,)), dma((4, n)), dma((1,)), dma((n,)), dma((1,)), dma((n,)),
         ],
         compiler_params=pltpu.CompilerParams(
-            collective_id=0, has_side_effects=True, vmem_limit_bytes=52 * 2**20
+            collective_id=0, has_side_effects=True, vmem_limit_bytes=54 * 2**20
         ),
         name="whole",
     )(

time: 126 us -> 117 us (0.929)
  Pallas kernels: 123 us -> 114 us
    pallas_call x1, Pallas kernels: 123 us -> 114 us  [on_device(): pl.pallas_call(whole_kernel, out_shape=(pltpu.VMEM((new, heads * LATENT),...]
where the time goes in v1:
time: 117 us
  Pallas kernels  114 us (97%)
  local copies, waits for them, and re-layouts  1.97 us (2%)
  between operations  1.29 us (1%)
    pallas_call x1, Pallas kernels, on_device(): pl.pallas_call(whole_kernel, out_shape=(pltpu.VMEM((new, heads * LATENT),...  114 us

profile of v1, /device:TPU:1, one launch (start us, length us, event | category | flops | bytes accessed | tf_op | source)
XLA Modules:
  0.0 116.9 jit_solution(8339253704572574713)
XLA Ops:
  1.3 113.7 %whole.1 = (bf16[128,8192]{1,0:T(8,128)(2,1)S(1)}, bf16[16,3584]{1,0:T(8,128)(2,1)S(1)}) custom-call(s32[1]{0:T(128)S(6)} %copy.18.length, s32[8,16]{1,0:T(8,128)} %bitcast.4, f32[8,16]{1,0:T(8,128)} %bitcast.5, s32[1,32]{1,0:T(1,128)} %owner.1, s32[1,32]{1,0:T(1,128)} %slot.1, bf16[16,3584]{1,0:T(8,128)(2,1)} %tokens.1, bf16[8,36864]{1,0:T(8,128)(2,1)} %pool_hbm.1, ...), custom_call_target="tpu_custom_call" | custom-call | tf_op jit(solution)/shard_map/whole/pallas_call | solution.py:551
  115.0 1.3 %copy.16 = bf16[128,8192]{1,0:T(8,128)(2,1)} copy(bf16[128,8192]{1,0:T(8,128)(2,1)S(1)} %get-tuple-element.2) | data formatting | bytes 4194304
  116.3 0.6 copy.17

commit v2 on v1

--- a/solution.py
+++ b/solution.py
@@ -55,6 +55,10 @@
     return (x, z, g), (along_x, along_z, along_g)
 
 
+def farthest_first(i):
+    return 4 + (i >> 1) * (2 * (i & 1) - 1)
+
+
 def greet(along_x, along_z, along_g):
     barrier = pltpu.get_barrier_semaphore()
 
@@ -62,8 +66,8 @@
         pl.semaphore_signal(barrier, inc=1, device_id=dev, device_id_type=MESH)
 
     def one(d, carry):
-        signal(along_z(d)[1])
-        signal(along_g(d)[1])
+        signal(along_z(farthest_first(d))[1])
+        signal(along_g(farthest_first(d))[1])
         return carry
 
     lax.fori_loop(1, 8, one, 0)
@@ -78,7 +82,7 @@
 
 def exchange(src, dst, cols, me, along, send_sem, recv_sem):
     def one(d, carry):
-        other, dev = along(d)
+        other, dev = along(farthest_first(d))
         pltpu.make_async_remote_copy(
             src_ref=src.at[block_at(other), cols],
             dst_ref=dst.at[block_at(me), cols],
@@ -152,8 +156,9 @@
 
 
 def whole_kernel(
-    length, ids, gates, owner, slot, tokens, pool_hbm, wg_hbm, wu_hbm, wd_hbm, q_hbm, suffix,
+    length, ids_hbm, gates_hbm, owner_hbm, slot_hbm, tokens_hbm, pool_hbm, wg_hbm, wu_hbm, wd_hbm, q_hbm, suffix_hbm,
     context, out,
+    ids, gates, owner, slot, tokens, suffix,
     rows, za, zb, xg, pool, ps, pza, pzb, pya, kg, wg, wu, wd, hidden,
     queries, qx, keys, causal, partial, stats,
     part_far, part_right, part_left, near_right, near_left, part_own, relay_left, relay_right, from_left, from_right,
@@ -163,6 +168,14 @@
     (x, z, g), (along_x, along_z, along_g) = peers()
     greeted = greet(along_x, along_z, along_g)
     bf, f32 = jnp.bfloat16, jnp.float32
+    small = [
+        pltpu.make_async_copy(src, dst, local.at[6 + i])
+        for i, (src, dst) in enumerate(
+            ((ids_hbm, ids), (tokens_hbm, tokens), (owner_hbm, owner), (slot_hbm, slot), (gates_hbm, gates), (suffix_hbm, suffix))
+        )
+    ]
+    for load in small:
+        load.start()
     half_page = pool.shape[2]
     loads = [
         pltpu.make_async_copy(
@@ -194,6 +207,7 @@
     perm = regroup()
     top, low = slice(0, 64), slice(64, 128)
 
+    small[0].wait()
     expert = row_device((ROWS, tok_count), 0, True)
     hits = [ids[k : k + 1, :] == expert for k in range(ids.shape[0])]
     named = hits[0]
@@ -202,18 +216,29 @@
     below = (iota((tok_count, tok_count), 0) < iota((tok_count, tok_count), 1)).astype(f32).astype(bf)
     before = mm(named.astype(f32).astype(bf), below)
     placed = named & (before == (iota((ROWS, tok_count), 0) & 1).astype(f32))
+    placing = placed.astype(f32).astype(bf)
+    small[1].wait()
+
+    def z_send(c):
+        rows[:, own[c]] = mm(placing, tokens[:, own[c]]).astype(bf)
+        exchange(rows, za, out_chunks[c], z, along_z, zs.at[0], zr.at[c])
+
+    greeted()
+    z_send(0)
     page_count = owner.shape[1]
+    small[2].wait()
+    small[3].wait()
     asks = owner[...] == row_device((ROWS, page_count), 0, True)
     asked = jnp.sum(jnp.where(asks, slot[...] + 1, 0), axis=1, keepdims=True)
     lane = iota((ROWS, REQ), 1)
     row = iota((ROWS, REQ), 0)
     req = (lane < 16) & ((lane & 7) + 1 == asked) & ((lane >> 3) == (row & 1))
     rows[:, hid:] = req.astype(f32).astype(bf)
-    rows[:, 0:hid] = mm(placed.astype(f32).astype(bf), tokens[...]).astype(bf)
-    greeted()
-    for c in range(len(out_chunks)):
-        exchange(rows, za, out_chunks[c], z, along_z, zs.at[0], zr.at[c])
-
+    for c in range(1, len(own)):
+        z_send(c)
+
+    small[4].wait()
+    small[5].wait()
     weight = jnp.zeros((ROWS, tok_count), f32)
     for k, hit in enumerate(hits):
         weight = weight + jnp.where(hit & placed, gates[k : k + 1, :], 0.0)
@@ -222,7 +247,7 @@
     gate_2 = rest.astype(bf)
     gate_3 = (rest - gate_2.astype(f32)).astype(bf)
     eye = identity(tok_count)
-    gate_1, gate_2, gate_3 = (nt(eye, part).astype(bf) for part in (gate_1, gate_2, gate_3))
+    gate_parts = jnp.concatenate([nt(eye, part) for part in (gate_1, gate_2, gate_3)], axis=0).astype(bf)
     holds = (owner[...] == row_device((ROWS, page_count), 0, False)).astype(f32).astype(bf)
     spread = ((iota((64, page_count), 0) >> 1) == iota((64, page_count), 1)).astype(f32).astype(bf)
     sel = jnp.where((iota((64, ROWS), 0) & 1) == (iota((64, ROWS), 1) & 1), nt(spread, holds), 0.0).astype(bf)
@@ -324,7 +349,9 @@
     def combine(c):
         settle(cza, cols[c], czr.at[c])
         back = cza[:, cols[c]]
-        out[:, cols[c]] = (mm(gate_1, back) + mm(gate_2, back) + mm(gate_3, back)).astype(bf)
+        sums = mm(gate_parts, back)
+        n = tok_count
+        out[:, cols[c]] = (sums[0:n] + sums[n : 2 * n] + sums[2 * n :]).astype(bf)
 
     def place_queries():
         loads[5].wait()
@@ -490,14 +517,15 @@
         relay(4)
         to_y(3)
 
-    @pl.loop(0, 8)
+    @pl.loop(0, 4)
     def _(i):
-        attend_first(i)
+        attend_first(2 * i)
+        attend_first(2 * i + 1)
         pl.when(i == 0)(first_0)
-        pl.when(i == 1)(first_1)
-        pl.when(i == 3)(first_3)
-        pl.when(i == 5)(first_5)
-        pl.when(i == 6)(first_6)
+        pl.when(i == 0)(first_1)
+        pl.when(i == 1)(first_3)
+        pl.when(i == 2)(first_5)
+        pl.when(i == 3)(first_6)
 
     page_forward(3)
     to_z(2)
@@ -513,11 +541,12 @@
     def second_4():
         combine(2)
 
-    @pl.loop(0, 8)
+    @pl.loop(0, 4)
     def _(i):
-        attend_second(i)
-        pl.when(i == 1)(second_1)
-        pl.when(i == 4)(second_4)
+        attend_second(2 * i)
+        attend_second(2 * i + 1)
+        pl.when(i == 0)(second_1)
+        pl.when(i == 2)(second_4)
 
     combine(3)
     combine(4)
@@ -545,6 +574,7 @@
     hbm = pl.BlockSpec(memory_space=pltpu.HBM)
     dma = pltpu.SemaphoreType.DMA
     d, p, n = len(DISPATCH), len(PAGES), len(COMBINE)
+    ids, gates, suffix = expert_ids.T, gate_weights.T, suffix_latent.T
     new, heads = queries.shape[0], queries.shape[1] // KD
     full, paged = pltpu.VMEM((ROWS, hid), bf), pltpu.VMEM((ROWS, wide), bf)
     asking = pltpu.VMEM((ROWS, REQ + hid), bf)
@@ -554,9 +584,10 @@
             pltpu.VMEM((new, heads * LATENT), bf),
             pltpu.VMEM(moe_input.shape, bf),
         ),
-        in_specs=[pl.BlockSpec(memory_space=pltpu.SMEM)] + [vmem] * 5 + [hbm] * 5 + [vmem],
+        in_specs=[pl.BlockSpec(memory_space=pltpu.SMEM)] + [hbm] * 11,
         out_specs=(vmem, vmem),
         scratch_shapes=[
+            *(pltpu.VMEM(a.shape, a.dtype) for a in (ids, gates, page_owner, page_slot, moe_input, suffix)),
             asking, asking, asking,
             pltpu.VMEM((NX, ROWS, REQ + hid), bf),
             pltpu.VMEM((2, page_pool.shape[0], wide), bf),
@@ -573,7 +604,7 @@
             full, pltpu.VMEM((ROWS, hid), f32), pltpu.VMEM((ROWS, hid), f32), full, full, pltpu.VMEM((ROWS, hid), f32),
             pltpu.VMEM((64, hid), bf), pltpu.VMEM((64, hid), bf), full, full,
             full, full, full, full,
-            dma((6,)),
+            dma((12,)),
             dma((1,)), dma((d,)), dma((1,)), dma((d,)), dma((4,)), dma((3, d)),
             dma((1,)), dma((p,)), dma((1,)), dma((p,)), dma((4,)), dma((3, p)),
             dma((6,)), dma((4, n)), dma((1,)), dma((n,)), dma((1,)), dma((n,)),
@@ -583,8 +614,8 @@
         ),
         name="whole",
     )(
-        prefix_len, expert_ids.T, gate_weights.T, page_owner, page_slot, moe_input,
-        page_pool, w_gate, w_up, w_down, queries, suffix_latent.T,
+        prefix_len, ids, gates, page_owner, page_slot, moe_input,
+        page_pool, w_gate, w_up, w_down, queries, suffix,
     )
 
 

time: 117 us -> 115 us (0.983)
  Pallas kernels: 114 us -> 112 us
    pallas_call x1, Pallas kernels: 114 us -> 112 us  [on_device(): pl.pallas_call(whole_kernel, out_shape=(pltpu.VMEM((new, heads * LATENT),...]
where the time goes in v2:
time: 115 us
  Pallas kernels  112 us (97%)
  local copies, waits for them, and re-layouts  1.97 us (2%)
  between operations  1.29 us (1%)
    pallas_call x1, Pallas kernels, on_device(): pl.pallas_call(whole_kernel, out_shape=(pltpu.VMEM((new, heads * LATENT),...  112 us

profile of v2, /device:TPU:1, one launch (start us, length us, event | category | flops | bytes accessed | tf_op | source)
XLA Modules:
  0.0 115.3 jit_solution(558449857417565323)
XLA Ops:
  1.3 112.0 %whole.1 = (bf16[128,8192]{1,0:T(8,128)(2,1)S(1)}, bf16[16,3584]{1,0:T(8,128)(2,1)S(1)}) custom-call(s32[1]{0:T(128)S(6)} %copy.18.length, s32[8,16]{1,0:T(8,128)} %bitcast.4, f32[8,16]{1,0:T(8,128)} %bitcast.5, s32[1,32]{1,0:T(1,128)} %owner_hbm.1, s32[1,32]{1,0:T(1,128)} %slot_hbm.1, bf16[16,3584]{1,0:T(8,128)(2,1)} %tokens_hbm.1, ...), custom_call_target="tpu_custom_call" | custom-call | tf_op jit(solution)/shard_map/whole/pallas_call | solution.py:581
  113.3 1.3 %copy.16 = bf16[128,8192]{1,0:T(8,128)(2,1)} copy(bf16[128,8192]{1,0:T(8,128)(2,1)S(1)} %get-tuple-element.2) | data formatting | bytes 4194304
  114.6 0.6 copy.17

commit v3 on v2

--- a/solution.py
+++ b/solution.py
@@ -259,15 +259,17 @@
 
     def y_to_x(c):
         settle(mine, out_chunks[c], yr.at[c])
-        part = xg.at[x, :, own[c]]
-        send(part, part, xs.at[0], xr.at[0, c], to_right)
-        send(part, part, xs.at[1], xr.at[1, c], to_left)
+        upper, lower = xg.at[x, top, own[c]], xg.at[x, low, own[c]]
+        send(upper, upper, xs.at[0], xr.at[0, c], to_right)
+        send(lower, lower, xs.at[1], xr.at[1, c], to_left)
+        send(lower, lower, xs.at[0], xr.at[3, c], to_right)
+        send(upper, upper, xs.at[1], xr.at[4, c], to_left)
 
     def forward(c):
-        arrived(xg.at[left, :, own[c]], xr.at[0, c])
+        arrived(xg.at[left, top, own[c]], xr.at[0, c])
         part = xg.at[left, top, own[c]]
         send(part, part, xs.at[2], xr.at[2, 0], to_right)
-        arrived(xg.at[right, :, own[c]], xr.at[1, c])
+        arrived(xg.at[right, low, own[c]], xr.at[1, c])
         part = xg.at[right, low, own[c]]
         send(part, part, xs.at[3], xr.at[2, 0], to_left)
 
@@ -460,8 +462,12 @@
     page_z_to_y(0)
     page_z_to_y(1)
     forward(4)
+    for c in range(len(own)):
+        arrived(xg.at[right, top, own[c]], xr.at[4, c])
     ffn(right)
     page_y_to_x(0)
+    for c in range(len(own)):
+        arrived(xg.at[left, low, own[c]], xr.at[3, c])
     ffn(left)
     page_z_to_y(2)
     page_y_to_x(1)
@@ -605,7 +611,7 @@
             pltpu.VMEM((64, hid), bf), pltpu.VMEM((64, hid), bf), full, full,
             full, full, full, full,
             dma((12,)),
-            dma((1,)), dma((d,)), dma((1,)), dma((d,)), dma((4,)), dma((3, d)),
+            dma((1,)), dma((d,)), dma((1,)), dma((d,)), dma((4,)), dma((5, d)),
             dma((1,)), dma((p,)), dma((1,)), dma((p,)), dma((4,)), dma((3, p)),
             dma((6,)), dma((4, n)), dma((1,)), dma((n,)), dma((1,)), dma((n,)),
         ],

time: 115 us -> 115 us (level)
  no operation moved by 1% of the time
where the time goes in v3:
time: 115 us
  Pallas kernels  112 us (97%)
  local copies, waits for them, and re-layouts  1.97 us (2%)
  between operations  1.29 us (1%)
    pallas_call x1, Pallas kernels, on_device(): pl.pallas_call(whole_kernel, out_shape=(pltpu.VMEM((new, heads * LATENT),...  112 us

profile of v3, /device:TPU:1, one launch (start us, length us, event | category | flops | bytes accessed | tf_op | source)
XLA Modules:
  0.0 115.3 jit_solution(8030959488221136387)
XLA Ops:
  1.3 112.0 %whole.1 = (bf16[128,8192]{1,0:T(8,128)(2,1)S(1)}, bf16[16,3584]{1,0:T(8,128)(2,1)S(1)}) custom-call(s32[1]{0:T(128)S(6)} %copy.18.length, s32[8,16]{1,0:T(8,128)} %bitcast.4, f32[8,16]{1,0:T(8,128)} %bitcast.5, s32[1,32]{1,0:T(1,128)} %owner_hbm.1, s32[1,32]{1,0:T(1,128)} %slot_hbm.1, bf16[16,3584]{1,0:T(8,128)(2,1)} %tokens_hbm.1, ...), custom_call_target="tpu_custom_call" | custom-call | tf_op jit(solution)/shard_map/whole/pallas_call | solution.py:587
  113.3 1.3 %copy.16 = bf16[128,8192]{1,0:T(8,128)(2,1)} copy(bf16[128,8192]{1,0:T(8,128)(2,1)S(1)} %get-tuple-element.2) | data formatting | bytes 4194304
  114.6 0.6 copy.17
